TPU v7x, 128 devices: a whole 4x4x4 slice. The times are simulated.
128 devices in a mesh: gx: 16 (over y, x), yz: 8 (over z, core).
Axes of the slice: x: 4, y: 4, z: 4, core: 2. Of those that a mesh axis runs over, the one named last changes fastest.
Arguments:
- fields: bfloat16 [4, 512, 262144], P(None, 'gx', 'yz'), may hold values from -8 to 8
- test_matrix: float32 [512, 64], replicated, may hold values from -6 to 6
Outputs:
- factor: float32 [512, 64], replicated
- core: bfloat16 [64, 4, 262144], P('gx', None, 'yz')
All inputs are finite; a program needn't handle non-finite values.
Results may differ from a plain program's by a relative error of at most 0.0036.
Values may be sent and summed in bfloat16 or wider, within the bound.
No kernel may reach another device: no remote copies, remote signals or barrier semaphores. Data moves between devices by JAX's collectives and lax.ppermute only.
A program may use at most 192 MiB of HBM per device.

v0:
```python
import jax
import jax.numpy as jnp
from jax import lax
from jax.sharding import PartitionSpec as P


def orthonormal(matrix_y):
    moment = jnp.dot(matrix_y.T, matrix_y, precision=lax.Precision.HIGHEST)
    lower = jnp.linalg.cholesky(moment)
    return lax.linalg.triangular_solve(
        lower, matrix_y, left_side=False, lower=True, transpose_a=True
    )


def body(fields, test_matrix):
    species_count, slab_len, cell_count = fields.shape
    norm_scale = 1.0 / (species_count * cell_count * lax.axis_size("yz"))
    pieces = lax.all_to_all(fields, "gx", split_axis=2, concat_axis=1, tiled=True)
    gram_parts = jnp.einsum("sxc,syc->sxy", pieces, pieces, preferred_element_type=jnp.float32)
    gram_parts, fibres = (gram_parts, pieces)
    local_gram = jnp.sum(gram_parts, axis=0)
    summed_gram = lax.psum(local_gram, ("gx", "yz"))
    sketch = jnp.dot(summed_gram, test_matrix, precision=lax.Precision.HIGHEST) * norm_scale
    factor = orthonormal(orthonormal(sketch))
    factor_low = factor.astype(jnp.bfloat16)
    core_block = jnp.einsum(
        "xr,sxc->rsc", factor_low, fibres, preferred_element_type=jnp.float32
    ).astype(jnp.bfloat16)
    core_block = lax.all_to_all(core_block, "gx", split_axis=0, concat_axis=2, tiled=True)
    return (factor, core_block)


def solution(mesh):
    in_specs = (P(None, "gx", "yz"), P())
    out_specs = (P(), P("gx", None, "yz"))
    return jax.shard_map(body, mesh=mesh, in_specs=in_specs, out_specs=out_specs, check_vma=False)
```

profile of v0, /device:TPU:0, one launch (start us, length us, event | category | flops | bytes accessed | tf_op | source)
XLA Modules:
  0.0 475.0 jit_solution(1052672916725822940)
XLA Ops:
  7.2 0.0 copy-start
  7.2 0.0 all-reduce.2.cloned.1.call-start
  7.2 39.0 %copy.8 = bf16[4,32,32768]{1,0,2:T(4,128)(2,1)} copy(bf16[4,32,32768]{2,1,0:T(8,128)(2,1)} %param.5) | data formatting | bytes 16777216 | tf_op args[0]
  46.2 35.0 %reshape.23 = bf16[16,2,131072]{2,1,0:T(2,128)(2,1)} reshape(bf16[32768,4,32]{2,1,0:T(4,128)(2,1)} %bitcast.50) | data formatting | bytes 16777216
  81.3 103.0 %all_to_all.36 = bf16[16,2,131072]{2,1,0:T(2,128)(2,1)} all-to-all(bf16[16,2,131072]{2,1,0:T(2,128)(2,1)} %reshape.23), channel_id=1, replica_groups=mesh['gx'=16,'yz'=8] {'gx'}, dimensions={0} | all-to-all | bytes 16777216 | tf_op jit(solution)/shard_map/all_to_all | solution.py:18
  184.3 22.9 %reshape.24 = bf16[32768,4,32]{2,1,0:T(4,128)(2,1)} reshape(bf16[16,2,131072]{2,1,0:T(2,128)(2,1)} %all_to_all.36) | data formatting | bytes 16777216
  207.2 45.2 %copy.9 = bf16[4,32,16,2048]{3,1,2,0:T(8,128)(2,1)} copy(bf16[4,32,16,2048]{1,0,3,2:T(4,128)(2,1)} %bitcast.49) | data formatting | bytes 16777216 | tf_op jit(solution)/shard_map/all_to_all | solution.py:18
  252.4 11.3 %convolution_bitcast_fusion = f32[512,512]{1,0:T(8,128)} fusion(bf16[4,512,2048]{2,1,0:T(8,128)(2,1)} %bitcast.51), kind=kOutput, calls=%fused_computation.1 | convolution fusion | flops 4294967296 | bytes 9437184 | tf_op jit(solution)/shard_map/sxc,syc->sxy/dot_general | solution.py:19
  263.7 0.0 all-reduce.2.cloned.1.call-update
  263.7 146.2 %all-reduce.2.cloned.1.call-done = f32[512,512]{1,0:T(8,128)} async-done(((f32[512,512]{1,0:T(8,128)}), f32[512,512]{1,0:T(8,128)}) %all-reduce.2.cloned.1.call-update) | async-done | bytes 1048592 | tf_op jit(solution)/shard_map/psum | solution.py:22
  409.9 0.0 copy-done
  409.9 2.4 convolution_multiply_fusion
  412.3 0.3 fusion.10
  412.5 0.1 copy.10
  412.6 5.8 %cholesky.44 = f32[64,64]{1,0:T(8,128)S(1)} custom-call(f32[64,64]{1,0:T(8,128)S(1)} %fusion.7), custom_call_target="Cholesky" | custom-call | tf_op jit(solution)/shard_map/jit(cholesky)/cholesky | solution.py:9
  418.5 0.6 compare_reduce_fusion.1
  419.1 0.7 fusion.2
  419.8 4.9 %custom-call.6 = f32[1,64,64]{1,2,0:T(8,128)S(1)} custom-call(f32[1,64,64]{2,1,0:T(8,128)S(1)} %fusion.2), custom_call_target="InvertDiagBlocksLowerTriangular" | custom-call | tf_op jit(solution)/shard_map/triangular_solve/custom-call.0 | solution.py:10
  424.7 0.3 convolution_bitcast_fusion.2
  425.0 0.3 fusion.11
  425.3 0.1 copy.11
  425.4 5.8 %cholesky.55 = f32[64,64]{1,0:T(8,128)S(1)} custom-call(f32[64,64]{1,0:T(8,128)S(1)} %fusion.5), custom_call_target="Cholesky" | custom-call | tf_op jit(solution)/shard_map/jit(cholesky)/cholesky | solution.py:9
  431.3 0.6 compare_reduce_fusion
  431.9 0.7 fusion.3
  432.6 4.9 %custom-call.7 = f32[1,64,64]{1,2,0:T(8,128)S(1)} custom-call(f32[1,64,64]{2,1,0:T(8,128)S(1)} %fusion.3), custom_call_target="InvertDiagBlocksLowerTriangular" | custom-call | tf_op jit(solution)/shard_map/triangular_solve/custom-call.0 | solution.py:10
  437.5 0.3 convolution_bitcast_fusion.1
  437.8 0.0 copy-start.1
  437.8 5.0 %convolution_convert_fusion = bf16[64,4,2048]{2,0,1:T(8,128)(2,1)S(1)} fusion(bf16[4,512,2048]{2,1,0:T(8,128)(2,1)} %bitcast.52, f32[512,64]{0,1:T(8,128)S(1)} %convolution_bitcast_fusion.1), kind=kOutput, calls=%fused_computation | convolution fusion | flops 537427968 | bytes 9568256 | tf_op jit(solution)/shard_map/xr,sxc->rsc/dot_general | solution.py:26
  442.9 0.8 copy.12
  443.7 23.0 %all_to_all.37 = bf16[64,4,2048]{2,1,0:T(4,128)(2,1)S(1)} all-to-all(bf16[64,4,2048]{2,1,0:T(4,128)(2,1)S(1)} %copy.12), channel_id=1, replica_groups=mesh['gx'=16,'yz'=8] {'gx'}, dimensions={0} | all-to-all | bytes 2097152 | tf_op jit(solution)/shard_map/all_to_all | solution.py:29
  466.7 1.4 copy.14
  468.1 0.0 copy-done.1
  (4 shorter events, 0.1 us)
Async XLA Ops:
  7.2 402.7 %copy-start = (f32[512,64]{0,1:T(8,128)S(1)}, f32[512,64]{0,1:T(8,128)}, u32[]{:S(2)}) copy-start(f32[512,64]{0,1:T(8,128)} %param.6) | copy-start | bytes 393220
  7.2 402.7 %all-reduce.2.cloned.1.call-start = ((), (), s32[]{:S(2)}) async-start(), calls=%async_computation.2 | async-start | bytes 2097152 | tf_op jit(solution)/shard_map/psum | solution.py:22
  437.8 30.3 %copy-start.1 = (f32[512,64]{0,1:T(8,128)}, f32[512,64]{0,1:T(8,128)S(1)}, u32[]{:S(2)}) copy-start(f32[512,64]{0,1:T(8,128)S(1)} %convolution_bitcast_fusion.1) | copy-start | bytes 393220
Sparse Core Ops, SparseCore 0:
  263.8 145.9 all-reduce.1
where the time goes:
time: 478 us; the launch traced here: 475 us
  waiting for transfers between devices  146 us (31%)
  local copies, waits for them, and re-layouts  145 us (30%)
  blocking collectives  126 us (26%)
  other arithmetic  24.2 us (5%)
  matrix products  19.8 us (4%)
  between operations  14.1 us (3%)
    psum x1, waiting for transfers between devices, body(): summed_gram = lax.psum(local_gram, ('gx', 'yz'))  146 us
    all_to_all x1, blocking collectives, body(): lax.all_to_all(fields, 'gx', split_axis=2, concat_axis=1, tiled=True)  103 us
    unnamed x7, local copies, waits for them, and re-layouts  97 us
    all_to_all x1, local copies, waits for them, and re-layouts, body(): lax.all_to_all(fields, 'gx', split_axis=2, concat_axis=1, tiled=True)  45.2 us
    all_to_all x1, blocking collectives, body(): lax.all_to_all(core_block, 'gx', split_axis=0, concat_axis=2, tiled=True)  23 us
    another operation x6, other arithmetic, orthonormal(): lower = jnp.linalg.cholesky(moment)  13 us
    dot_general x1, matrix products, body(): jnp.einsum('sxc,syc->sxy', pieces, pieces, preferred_element_type=jnp.flo...  11.3 us
    another operation x4, other arithmetic, orthonormal(): lax.linalg.triangular_solve(lower, matrix_y, left_side=False, lower=True,...  11.1 us
  transfers between devices with their start and end apart: 1, of which 1 were waited for; matrix products, arithmetic and copies ran while one was open for 0% of the time, Pallas kernels for 0%

commit v1 on v0

--- a/solution.py
+++ b/solution.py
@@ -19,7 +19,7 @@
     gram_parts = jnp.einsum("sxc,syc->sxy", pieces, pieces, preferred_element_type=jnp.float32)
     gram_parts, fibres = (gram_parts, pieces)
     local_gram = jnp.sum(gram_parts, axis=0)
-    summed_gram = lax.psum(local_gram, ("gx", "yz"))
+    summed_gram = jnp.sum(lax.all_gather(local_gram, ("gx", "yz")), axis=0)
     sketch = jnp.dot(summed_gram, test_matrix, precision=lax.Precision.HIGHEST) * norm_scale
     factor = orthonormal(orthonormal(sketch))
     factor_low = factor.astype(jnp.bfloat16)

time: 478 us -> 654 us (1.37)
  waiting for transfers between devices: 146 us -> 282 us
  other arithmetic: 24.2 us -> 64.9 us
    all_gather x0 -> x1, waiting for transfers between devices: none -> 282 us  [body(): summed_gram = jnp.sum(lax.all_gather(local_gram, ('gx', 'yz')), axis=0)]
    psum x1 -> x0, waiting for transfers between devices: 146 us -> none  [body(): summed_gram = lax.psum(local_gram, ('gx', 'yz'))]
    reduce_sum x0 -> x1, other arithmetic: none -> 40.7 us  [body(): summed_gram = jnp.sum(lax.all_gather(local_gram, ('gx', 'yz')), axis=0)]
where the time goes in v1:
time: 654 us; the launch traced here: 651 us
  waiting for transfers between devices  282 us (43%)
  local copies, waits for them, and re-layouts  145 us (22%)
  blocking collectives  127 us (19%)
  other arithmetic  64.9 us (10%)
  matrix products  18.6 us (3%)
  between operations  14.2 us (2%)
    all_gather x1, waiting for transfers between devices, body(): summed_gram = jnp.sum(lax.all_gather(local_gram, ('gx', 'yz')), axis=0)  282 us
    all_to_all x1, blocking collectives, body(): lax.all_to_all(fields, 'gx', split_axis=2, concat_axis=1, tiled=True)  103 us
    unnamed x7, local copies, waits for them, and re-layouts  97 us
    all_to_all x1, local copies, waits for them, and re-layouts, body(): lax.all_to_all(fields, 'gx', split_axis=2, concat_axis=1, tiled=True)  45.3 us
    reduce_sum x1, other arithmetic, body(): summed_gram = jnp.sum(lax.all_gather(local_gram, ('gx', 'yz')), axis=0)  40.7 us
    all_to_all x1, blocking collectives, body(): lax.all_to_all(core_block, 'gx', split_axis=0, concat_axis=2, tiled=True)  24.2 us
  transfers between devices with their start and end apart: 1, of which 1 were waited for; matrix products, arithmetic and copies ran while one was open for 0% of the time, Pallas kernels for 0%

profile of v1, /device:TPU:0, one launch (start us, length us, event | category | flops | bytes accessed | tf_op | source)
XLA Modules:
  0.0 651.4 jit_solution(11102270385642201909)
XLA Ops:
  7.2 0.0 copy-start
  7.2 0.0 all-gather.3.cloned.1.call-start
  7.2 39.0 %copy.8 = bf16[4,32,32768]{1,0,2:T(4,128)(2,1)} copy(bf16[4,32,32768]{2,1,0:T(8,128)(2,1)} %param.5) | data formatting | bytes 16777216 | tf_op args[0]
  46.2 35.0 %reshape.24 = bf16[16,2,131072]{2,1,0:T(2,128)(2,1)} reshape(bf16[32768,4,32]{2,1,0:T(4,128)(2,1)} %bitcast.51) | data formatting | bytes 16777216
  81.3 103.0 %all_to_all.36 = bf16[16,2,131072]{2,1,0:T(2,128)(2,1)} all-to-all(bf16[16,2,131072]{2,1,0:T(2,128)(2,1)} %reshape.24), channel_id=1, replica_groups=mesh['gx'=16,'yz'=8] {'gx'}, dimensions={0} | all-to-all | bytes 16777216 | tf_op jit(solution)/shard_map/all_to_all | solution.py:18
  184.3 22.9 %reshape.25 = bf16[32768,4,32]{2,1,0:T(4,128)(2,1)} reshape(bf16[16,2,131072]{2,1,0:T(2,128)(2,1)} %all_to_all.36) | data formatting | bytes 16777216
  207.2 45.3 %copy.9 = bf16[4,32,16,2048]{3,1,2,0:T(8,128)(2,1)} copy(bf16[4,32,16,2048]{1,0,3,2:T(4,128)(2,1)} %bitcast.50) | data formatting | bytes 16777216 | tf_op jit(solution)/shard_map/all_to_all | solution.py:18
  252.5 11.3 %convolution_bitcast_fusion = f32[512,512]{1,0:T(8,128)} fusion(bf16[4,512,2048]{2,1,0:T(8,128)(2,1)} %bitcast.52), kind=kOutput, calls=%fused_computation.1 | convolution fusion | flops 4294967296 | bytes 9437184 | tf_op jit(solution)/shard_map/sxc,syc->sxy/dot_general | solution.py:19
  263.7 0.0 all-gather.3.cloned.1.call-update
  263.8 281.9 %all-gather.3.cloned.1.call-done = f32[65536,512]{1,0:T(8,128)} async-done(((f32[512,512]{1,0:T(8,128)}), f32[65536,512]{1,0:T(8,128)}) %all-gather.3.cloned.1.call-update) | async-done | bytes 134217744 | tf_op jit(solution)/shard_map/all_gather | solution.py:22
  545.7 40.7 %reduce_sum.8 = f32[512,512]{1,0:T(8,128)S(1)} reduce(f32[128,512,512]{2,1,0:T(8,128)} %bitcast.4, f32[]{:T(128)} %constant.31.clone.1), dimensions={0}, to_apply=%region_0.0 | reduce | flops 33292288 | bytes 135266304 | tf_op jit(solution)/shard_map/reduce_sum | solution.py:22
  586.4 0.0 copy-done
  586.4 1.1 convolution_multiply_fusion
  587.5 0.3 fusion.10
  587.8 0.1 copy.10
  587.9 5.8 cholesky.44
  593.8 0.6 compare_reduce_fusion.1
  594.4 0.7 fusion.2
  595.1 4.9 custom-call.6
  600.0 0.3 convolution_bitcast_fusion.2
  600.3 0.3 fusion.11
  600.6 0.1 copy.11
  600.7 5.8 cholesky.55
  606.6 0.6 compare_reduce_fusion
  607.2 0.7 fusion.3
  607.9 4.9 custom-call.7
  612.8 0.3 convolution_bitcast_fusion.1
  613.1 0.0 copy-start.1
  613.1 5.0 convolution_convert_fusion
  618.1 0.8 copy.12
  619.0 24.2 %all_to_all.37 = bf16[64,4,2048]{2,1,0:T(4,128)(2,1)S(1)} all-to-all(bf16[64,4,2048]{2,1,0:T(4,128)(2,1)S(1)} %copy.12), channel_id=1, replica_groups=mesh['gx'=16,'yz'=8] {'gx'}, dimensions={0} | all-to-all | bytes 2097152 | tf_op jit(solution)/shard_map/all_to_all | solution.py:29
  643.1 1.4 copy.14
  644.6 0.0 copy-done.1
  (4 shorter events, 0.1 us)
Async XLA Ops:
  7.2 579.2 %copy-start = (f32[512,64]{0,1:T(8,128)S(1)}, f32[512,64]{0,1:T(8,128)}, u32[]{:S(2)}) copy-start(f32[512,64]{0,1:T(8,128)} %param.6) | copy-start | bytes 393220
  7.2 538.5 %all-gather.3.cloned.1.call-start = ((), (), s32[]{:S(2)}) async-start(), calls=%async_computation.2 | async-start | bytes 135266304 | tf_op jit(solution)/shard_map/all_gather | solution.py:22
  613.1 31.5 %copy-start.1 = (f32[512,64]{0,1:T(8,128)}, f32[512,64]{0,1:T(8,128)S(1)}, u32[]{:S(2)}) copy-start(f32[512,64]{0,1:T(8,128)S(1)} %convolution_bitcast_fusion.1) | copy-start | bytes 393220
Sparse Core Ops, SparseCore 0:
  263.9 281.7 all-gather.2
